TPU v7x, 256 devices: a whole 4x4x8 slice. The times are simulated.
256 devices in a mesh: section: 4 (over x_lo, core), row: 8 (over z), col: 8 (over x_hi, y).
Axes of the slice: x: 4 (x_hi: 2, x_lo: 2; x = x_hi * 2 + x_lo), y: 4, z: 8, core: 2. Of those that a mesh axis runs over, the one named last changes fastest.
Arguments:
- images: bfloat16 [4, 8, 80, 80, 512], P('section', None, 'row', 'col'), may hold values from -6 to 6
- block_in: bfloat16 [512, 256], replicated, may hold values from -0.25 to 0.25
- block_grouped_one: bfloat16 [1152, 256], replicated, may hold values from -0.1875 to 0.1875
- block_grouped_two: bfloat16 [1152, 256], replicated, may hold values from -0.1875 to 0.1875
- block_out: bfloat16 [256, 512], replicated, may hold values from -0.375 to 0.375
- trans_in: bfloat16 [512, 768], replicated, may hold values from -0.25 to 0.25
- trans_grouped_one: bfloat16 [1152, 768], replicated, may hold values from -0.1875 to 0.1875
- trans_grouped_two: bfloat16 [1152, 768], replicated, may hold values from -0.1875 to 0.1875
- trans_out: bfloat16 [768, 1536], replicated, may hold values from -0.21875 to 0.21875
- trans_short: bfloat16 [512, 1536], replicated, may hold values from -0.25 to 0.25
Outputs:
- features: bfloat16 [4, 8, 40, 40, 1536], P('section', 'row', 'col')
All inputs are finite; a program needn't handle non-finite values.
Results may differ from a plain program's by a relative error of at most 0.012.
Values may be sent and summed in bfloat16 or wider, within the bound.
A program may use at most 64 MiB of HBM per device.

v0:
```python
import jax
import jax.numpy as jnp
from jax import lax
from jax.sharding import PartitionSpec as P

GELU_GAIN = 1.7015
RESIDUAL_SCALE = 0.2
BETA_BLOCK = 0.9805
BETA_TRANSITION = 0.9623


def with_halo(block, sides, width):
    for axis, dim in sides:
        count = lax.axis_size(axis)
        forward = [(i, i + 1) for i in range(count - 1)]
        backward = [(target, source) for source, target in forward]
        low = lax.ppermute(
            lax.slice_in_dim(block, block.shape[dim] - width, None, axis=dim), axis, forward
        )
        high = lax.ppermute(lax.slice_in_dim(block, 0, width, axis=dim), axis, backward)
        block = jnp.concatenate([low, block, high], axis=dim)
    return block


def activate(values):
    return GELU_GAIN * jax.nn.gelu(values, approximate=True)


def matmul_rows(tensor, weight):
    shaped = tensor.shape
    result = jnp.dot(tensor.reshape(-1, shaped[-1]), weight, preferred_element_type=jnp.float32)
    return result.reshape(shaped[:-1] + (weight.shape[1],))


def group_conv(padded, weight, stride):
    lot_count, image_count, height, breadth, channels = padded.shape
    batches = lot_count * image_count
    merged = padded.reshape(batches, height, breadth, channels)
    group_width = weight.shape[0] // 9
    out_height = (height - 2) // stride
    out_breadth = (breadth - 2) // stride
    offset = stride - 1
    tap_list = []
    for row_tap in range(3):
        for col_tap in range(3):
            start_row = offset + row_tap
            start_col = offset + col_tap
            tap_list.append(
                lax.slice(
                    merged,
                    (0, start_row, start_col, 0),
                    (
                        batches,
                        start_row + stride * (out_height - 1) + 1,
                        start_col + stride * (out_breadth - 1) + 1,
                        channels,
                    ),
                    (1, stride, stride, 1),
                )
            )
    stacked = jnp.stack(tap_list, axis=3)
    groups = channels // group_width
    stacked = stacked.reshape(batches, out_height, out_breadth, 9, groups, group_width)
    kernel = weight.reshape(9, group_width, groups, group_width)
    result = jnp.einsum("nhwtgc,tcgd->nhwgd", stacked, kernel, preferred_element_type=jnp.float32)
    return result.reshape(lot_count, image_count, out_height, out_breadth, channels)


def plane_rims(tensor):
    return with_halo(tensor, (("row", 2), ("col", 3)), 1)


def strip_rims(tensor):
    padded = with_halo(tensor, (("col", 2),), 1)
    return jnp.pad(padded, ((0, 0), (0, 0), (0, 0), (1, 1), (0, 0)))


def relayout(tensor):
    return lax.all_to_all(
        lax.all_to_all(tensor, "row", split_axis=1, concat_axis=2, tiled=True),
        "col",
        split_axis=2,
        concat_axis=3,
        tiled=True,
    )


def transition(block_result, weights_all, rims):
    trans_in, trans_grouped_one, trans_grouped_two, trans_out, trans_short = weights_all
    lot_count, image_count, height, breadth, channels = block_result.shape
    pre_trans = (activate(block_result.astype(jnp.float32)) * BETA_TRANSITION).astype(jnp.bfloat16)
    pooled = pre_trans.astype(jnp.float32).reshape(
        lot_count, image_count, height // 2, 2, breadth // 2, 2, channels
    )
    pooled = jnp.mean(pooled, axis=(3, 5)).astype(jnp.bfloat16)
    trans_first = activate(matmul_rows(pre_trans, trans_in)).astype(jnp.bfloat16)
    trans_second = activate(group_conv(rims(trans_first), trans_grouped_one, 2)).astype(
        jnp.bfloat16
    )
    trans_third = activate(group_conv(rims(trans_second), trans_grouped_two, 1)).astype(
        jnp.bfloat16
    )
    result = matmul_rows(pooled, trans_short) + RESIDUAL_SCALE * matmul_rows(trans_third, trans_out)
    return result.astype(jnp.bfloat16)


def local(
    images,
    block_in,
    block_grouped_one,
    block_grouped_two,
    block_out,
    trans_in,
    trans_grouped_one,
    trans_grouped_two,
    trans_out,
    trans_short,
):
    pre_block = (activate(images.astype(jnp.float32)) * BETA_BLOCK).astype(jnp.bfloat16)
    first_mid = activate(matmul_rows(pre_block, block_in)).astype(jnp.bfloat16)
    second_mid = activate(group_conv(plane_rims(first_mid), block_grouped_one, 1)).astype(
        jnp.bfloat16
    )
    third_mid = activate(group_conv(plane_rims(second_mid), block_grouped_two, 1)).astype(
        jnp.bfloat16
    )
    block_result = (
        images.astype(jnp.float32) + RESIDUAL_SCALE * matmul_rows(third_mid, block_out)
    ).astype(jnp.bfloat16)
    weights_all = (trans_in, trans_grouped_one, trans_grouped_two, trans_out, trans_short)
    features = transition(relayout(block_result), weights_all, strip_rims)
    return features


def solution(mesh):
    in_specs = (P("section", None, "row", "col", None), P(), P(), P(), P(), P(), P(), P(), P(), P())
    out_specs = P("section", "row", "col", None, None)
    return jax.shard_map(local, mesh=mesh, in_specs=in_specs, out_specs=out_specs, check_vma=False)
```

profile of v0, /device:TPU:24, one launch (start us, length us, event | category | flops | bytes accessed | tf_op | source)
XLA Modules:
  0.0 262.1 jit_solution(8434279550433340408)
XLA Ops:
  0.0 1.9 fusion.47
  3.3 1.4 reshape.586
  6.1 2.4 reshape.587
  8.5 2.0 fusion.73
  10.5 3.8 %collective-permute-start = (bf16[1,8,1,10,256]{4,1,3,2,0:T(8,128)(2,1)S(1)}, bf16[1,8,1,10,256]{4,1,3,2,0:T(8,128)(2,1)S(1)}, u32[]{:S(2)}, u32[]{:S(2)}) collective-permute-start(bf16[1,8,1,10,256]{4,1,3,2,0:T(8,128)(2,1)S(1)} %get-tuple-element.40), channel_id=1, source_target_pairs={{0,8},{8,16},{16,24},{24,32},{32,40},{40,48},{48,56},{1,9},{9,17},... | collective-permute-start | bytes 122888 | tf_op jit(solution)/shard_map/ppermute | solution.py:17
  16.0 4.2 %collective-permute-done.1 = bf16[1,8,1,10,256]{4,1,3,2,0:T(8,128)(2,1)S(1)} collective-permute-done((bf16[1,8,1,10,256]{4,1,3,2,0:T(8,128)(2,1)S(1)}, bf16[1,8,1,10,256]{4,1,3,2,0:T(8,128)(2,1)S(1)}, u32[]{:S(2)}, u32[]{:S(2)}) %collective-permute-start.1) | collective-permute-done | bytes 40992 | tf_op jit(solution)/shard_map/ppermute | solution.py:20
  20.9 4.6 %collective-permute-start.2 = (bf16[1,8,12,1,256]{4,1,3,2,0:T(8,128)(2,1)}, bf16[1,8,12,1,256]{4,1,3,2,0:T(8,128)(2,1)S(1)}, u32[]{:S(2)}, u32[]{:S(2)}) collective-permute-start(bf16[1,8,12,1,256]{4,1,3,2,0:T(8,128)(2,1)} %get-tuple-element.36), channel_id=1, source_target_pairs={{0,1},{1,2},{2,3},{3,4},{4,5},{5,6},{6,7},{8,9},{9,10},{10,11},{11... | collective-permute-start | bytes 147464 | tf_op jit(solution)/shard_map/ppermute | solution.py:17
  25.5 1.9 collective-permute-start.3
  28.3 6.9 %collective-permute-done.3 = bf16[1,8,12,1,256]{4,1,3,2,0:T(8,128)(2,1)S(1)} collective-permute-done((bf16[1,8,12,1,256]{4,1,3,2,0:T(8,128)(2,1)}, bf16[1,8,12,1,256]{4,1,3,2,0:T(8,128)(2,1)S(1)}, u32[]{:S(2)}, u32[]{:S(2)}) %collective-permute-start.3) | collective-permute-done | bytes 49184 | tf_op jit(solution)/shard_map/ppermute | solution.py:20
  37.7 1.7 convolution_bitcast_fusion.1
  40.1 3.8 %collective-permute-start.4 = (bf16[1,8,1,10,256]{4,1,3,2,0:T(8,128)(2,1)S(1)}, bf16[1,8,1,10,256]{4,1,3,2,0:T(8,128)(2,1)S(1)}, u32[]{:S(2)}, u32[]{:S(2)}) collective-permute-start(bf16[1,8,1,10,256]{4,1,3,2,0:T(8,128)(2,1)S(1)} %get-tuple-element.38), channel_id=1, source_target_pairs={{0,8},{8,16},{16,24},{24,32},{32,40},{40,48},{48,56},{1,9},{9,17},... | collective-permute-start | bytes 122888 | tf_op jit(solution)/shard_map/ppermute | solution.py:17
  45.6 5.3 %collective-permute-done.5 = bf16[1,8,1,10,256]{4,1,3,2,0:T(8,128)(2,1)S(1)} collective-permute-done((bf16[1,8,1,10,256]{4,1,3,2,0:T(8,128)(2,1)S(1)}, bf16[1,8,1,10,256]{4,1,3,2,0:T(8,128)(2,1)S(1)}, u32[]{:S(2)}, u32[]{:S(2)}) %collective-permute-start.5) | collective-permute-done | bytes 40992 | tf_op jit(solution)/shard_map/ppermute | solution.py:20
  51.5 1.9 collective-permute-start.6
  53.4 4.1 %collective-permute-start.7 = (bf16[1,8,12,1,256]{4,1,3,2,0:T(8,128)(2,1)}, bf16[1,8,12,1,256]{4,1,3,2,0:T(8,128)(2,1)S(1)}, u32[]{:S(2)}, u32[]{:S(2)}) collective-permute-start(bf16[1,8,12,1,256]{4,1,3,2,0:T(8,128)(2,1)} %get-tuple-element.35), channel_id=1, source_target_pairs={{1,0},{2,1},{3,2},{4,3},{5,4},{6,5},{7,6},{9,8},{10,9},{11,10},{12... | collective-permute-start | bytes 147464 | tf_op jit(solution)/shard_map/ppermute | solution.py:20
  58.5 4.7 %collective-permute-done.7 = bf16[1,8,12,1,256]{4,1,3,2,0:T(8,128)(2,1)S(1)} collective-permute-done((bf16[1,8,12,1,256]{4,1,3,2,0:T(8,128)(2,1)}, bf16[1,8,12,1,256]{4,1,3,2,0:T(8,128)(2,1)S(1)}, u32[]{:S(2)}, u32[]{:S(2)}) %collective-permute-start.7) | collective-permute-done | bytes 49184 | tf_op jit(solution)/shard_map/ppermute | solution.py:20
  65.7 1.7 convolution_bitcast_fusion
  68.5 35.7 %all_to_all.21 = bf16[1,8,10,10,512]{4,3,2,0,1:T(8,128)(2,1)} all-to-all(bf16[1,8,10,10,512]{4,3,2,0,1:T(8,128)(2,1)S(1)} %copy.260), channel_id=1, replica_groups=mesh['section'=4,'row'=8,'col'=8] {'row'}, dimensions={1} | all-to-all | bytes 1638400 | tf_op jit(solution)/shard_map/all_to_all | solution.py:80
  104.2 4.5 %all-to-all-start.1 = ((bf16[1,1,80,10,512]{4,3,1,0,2:T(8,128)(2,1)}), bf16[1,1,80,10,512]{4,3,1,0,2:T(8,128)(2,1)}, u32[]{:S(2)}, u32[]{:S(2)}) async-start(bf16[1,1,80,10,512]{4,3,1,0,2:T(8,128)(2,1)} %bitcast.160), calls=%async_computation.1 | async-start | bytes 2621440 | tf_op jit(solution)/shard_map/all_to_all | solution.py:79
  108.7 4.7 %reshape.597 = bf16[9,128,6,128]{3,2,1,0:T(8,128)(2,1)} reshape(bf16[1152,768]{1,0:T(8,128)(2,1)} %param.16) | data formatting | bytes 3538944 | tf_op jit(solution)/shard_map/reshape | solution.py:64
  113.4 4.7 %reshape.601 = bf16[9,128,6,128]{3,2,1,0:T(8,128)(2,1)} reshape(bf16[1152,768]{1,0:T(8,128)(2,1)} %param.17) | data formatting | bytes 3538944 | tf_op jit(solution)/shard_map/reshape | solution.py:64
  118.1 2.5 all-to-all-done.1
  120.6 4.4 %reshape.605 = f32[1,1,8,10,10,512]{5,1,4,3,2,0:T(1,128)} reshape(bf16[1,1,80,10,512]{4,3,1,0,2:T(8,128)(2,1)} %all-to-all-done.1) | data formatting | bytes 2457600 | tf_op jit(solution)/shard_map/convert_element_type | solution.py:91
  125.0 3.4 %copy.268 = f32[1,1,10,8,10,512]{5,4,3,2,1,0:T(8,128)} copy(f32[1,1,10,8,10,512]{5,1,4,2,3,0:T(1,128)} %bitcast.155) | data formatting | bytes 3276800 | tf_op jit(solution)/shard_map/convert_element_type | solution.py:91
  128.4 2.7 %copy.262 = f32[1,1,10,8,10,512]{5,1,4,3,2,0:T(1,128)} copy(f32[1,1,10,8,10,512]{5,1,4,2,3,0:T(1,128)S(1)} %bitcast.156) | data formatting | bytes 3276800 | tf_op jit(solution)/shard_map/convert_element_type | solution.py:91
  131.1 2.8 %reshape.604 = f32[800,512]{1,0:T(8,128)} reshape(f32[1,1,10,8,10,512]{5,4,3,2,1,0:T(8,128)} %copy.268) | data formatting | bytes 3276800 | tf_op jit(solution)/shard_map/convert_element_type | solution.py:91
  133.9 2.6 fusion.92
  137.3 4.5 %collective-permute-start.8 = (bf16[1,1,1,80,768]{4,3,2,1,0:T(8,128)(2,1)S(1)}, bf16[1,1,1,80,768]{4,3,2,1,0:T(8,128)(2,1)S(1)}, u32[]{:S(2)}, u32[]{:S(2)}) collective-permute-start(bf16[1,1,1,80,768]{4,3,2,1,0:T(8,128)(2,1)S(1)} %get-tuple-element.5), channel_id=1, source_target_pairs={{0,1},{1,2},{2,3},{3,4},{4,5},{5,6},{6,7},{8,9},{9,10},{10,11},{11... | collective-permute-start | bytes 368648 | tf_op jit(solution)/shard_map/ppermute | solution.py:17
  141.9 2.2 collective-permute-start.9
  145.5 6.8 %collective-permute-done.9 = bf16[1,1,1,80,768]{4,3,2,1,0:T(8,128)(2,1)S(1)} collective-permute-done((bf16[1,1,1,80,768]{4,3,2,1,0:T(8,128)(2,1)S(1)}, bf16[1,1,1,80,768]{4,3,2,1,0:T(8,128)(2,1)S(1)}, u32[]{:S(2)}, u32[]{:S(2)}) %collective-permute-start.9) | collective-permute-done | bytes 122912 | tf_op jit(solution)/shard_map/ppermute | solution.py:20
  152.3 1.6 fusion.51
  153.9 3.7 %slice.172 = bf16[1,5,40,768]{3,2,1,0:T(8,128)(2,1)} slice(bf16[1,12,82,768]{3,2,1,0:T(8,128)(2,1)} %fusion.51), slice={[0:1:1], [1:10:2], [1:80:2], [0:768:1]} | slice | bytes 614400 | tf_op jit(solution)/shard_map/slice | solution.py:49
  157.6 3.8 %slice.173 = bf16[1,5,40,768]{3,2,1,0:T(8,128)(2,1)} slice(bf16[1,12,82,768]{3,2,1,0:T(8,128)(2,1)} %fusion.51), slice={[0:1:1], [1:10:2], [2:81:2], [0:768:1]} | slice | bytes 614400 | tf_op jit(solution)/shard_map/slice | solution.py:49
  161.4 3.8 %slice.174 = bf16[1,5,40,768]{3,2,1,0:T(8,128)(2,1)} slice(bf16[1,12,82,768]{3,2,1,0:T(8,128)(2,1)} %fusion.51), slice={[0:1:1], [1:10:2], [3:82:2], [0:768:1]} | slice | bytes 614400 | tf_op jit(solution)/shard_map/slice | solution.py:49
  165.2 3.7 %slice.175 = bf16[1,5,40,768]{3,2,1,0:T(8,128)(2,1)} slice(bf16[1,12,82,768]{3,2,1,0:T(8,128)(2,1)} %fusion.51), slice={[0:1:1], [2:11:2], [1:80:2], [0:768:1]} | slice | bytes 614400 | tf_op jit(solution)/shard_map/slice | solution.py:49
  169.0 3.8 %slice.176 = bf16[1,5,40,768]{3,2,1,0:T(8,128)(2,1)} slice(bf16[1,12,82,768]{3,2,1,0:T(8,128)(2,1)} %fusion.51), slice={[0:1:1], [2:11:2], [2:81:2], [0:768:1]} | slice | bytes 614400 | tf_op jit(solution)/shard_map/slice | solution.py:49
  172.8 3.8 %slice.177 = bf16[1,5,40,768]{3,2,1,0:T(8,128)(2,1)} slice(bf16[1,12,82,768]{3,2,1,0:T(8,128)(2,1)} %fusion.51), slice={[0:1:1], [2:11:2], [3:82:2], [0:768:1]} | slice | bytes 614400 | tf_op jit(solution)/shard_map/slice | solution.py:49
  176.6 3.0 %slice.178 = bf16[1,5,40,768]{3,2,1,0:T(8,128)(2,1)S(1)} slice(bf16[1,12,82,768]{3,2,1,0:T(8,128)(2,1)} %fusion.51), slice={[0:1:1], [3:12:2], [1:80:2], [0:768:1]} | slice | bytes 614400 | tf_op jit(solution)/shard_map/slice | solution.py:49
  179.6 3.8 %slice.179 = bf16[1,5,40,768]{3,2,1,0:T(8,128)(2,1)} slice(bf16[1,12,82,768]{3,2,1,0:T(8,128)(2,1)} %fusion.51), slice={[0:1:1], [3:12:2], [2:81:2], [0:768:1]} | slice | bytes 614400 | tf_op jit(solution)/shard_map/slice | solution.py:49
  183.3 3.1 %slice.180 = bf16[1,5,40,768]{3,2,1,0:T(8,128)(2,1)S(1)} slice(bf16[1,12,82,768]{3,2,1,0:T(8,128)(2,1)} %fusion.51), slice={[0:1:1], [3:12:2], [3:82:2], [0:768:1]} | slice | bytes 614400 | tf_op jit(solution)/shard_map/slice | solution.py:49
  188.5 2.1 stack.141
  190.6 2.1 stack.142
  192.7 2.1 stack.143
  194.8 2.1 stack.144
  196.9 2.1 stack.145
  200.9 1.9 copy_dynamic-update-slice_fusion.34
  202.8 2.0 copy_dynamic-update-slice_fusion.33
  204.7 1.8 copy_dynamic-update-slice_fusion.32
  206.5 1.8 copy_dynamic-update-slice_fusion.31
  211.5 2.9 %fusion.54 = f32[1,5,40,6,128]{4,2,1,3,0:T(8,128)S(1)} fusion(bf16[9,128,6,128,1]{3,2,1,0,4:T(8,128)(2,1)S(1)} %bitcast.158, bf16[1,5,40,9,6,128]{5,2,3,1,4,0:T(8,128)(2,1)} %copy_dynamic-update-slice_fusion.27), kind=kOutput, calls=%fused_computation.70 | convolution fusion | flops 353894400 | bytes 5148672 | tf_op jit(solution)/shard_map/nhwtgc,tcgd->nhwgd/dot_general | solution.py:65
  216.8 1.9 collective-permute-start.10
  218.7 4.2 %collective-permute-start.11 = (bf16[1,1,1,40,768]{4,3,2,1,0:T(8,128)(2,1)S(1)}, bf16[1,1,1,40,768]{4,3,2,1,0:T(8,128)(2,1)S(1)}, u32[]{:S(2)}, u32[]{:S(2)}) collective-permute-start(bf16[1,1,1,40,768]{4,3,2,1,0:T(8,128)(2,1)S(1)} %get-tuple-element.43), channel_id=1, source_target_pairs={{1,0},{2,1},{3,2},{4,3},{5,4},{6,5},{7,6},{9,8},{10,9},{11,10},{12... | collective-permute-start | bytes 184328 | tf_op jit(solution)/shard_map/ppermute | solution.py:20
  222.9 3.1 %fusion.52 = f32[5,40,1536]{2,1,0:T(8,128)} fusion(bf16[512,1536]{1,0:T(8,128)(2,1)} %param.19, f32[5,40,512]{2,1,0:T(8,128)} %convert_reduce_fusion), kind=kOutput, calls=%fused_computation.64 | convolution fusion | flops 314777600 | bytes 3211264 | tf_op jit(solution)/shard_map/dot_general | solution.py:31
  226.0 2.4 collective-permute-done.11
  232.1 2.1 stack.151
  234.2 2.1 stack.152
  236.3 2.1 stack.153
  238.4 2.1 stack.154
  240.5 2.1 stack.155
  244.5 1.9 copy_dynamic-update-slice_fusion.25
  246.3 1.9 copy_dynamic-update-slice_fusion.24
  248.3 1.8 copy_dynamic-update-slice_fusion.23
  250.1 1.8 copy_dynamic-update-slice_fusion.22
  255.1 2.9 %fusion.59 = f32[1,5,40,6,128]{4,2,1,3,0:T(8,128)S(1)} fusion(bf16[9,128,6,128,1]{3,2,1,0,4:T(8,128)(2,1)S(1)} %bitcast.157, bf16[1,5,40,9,6,128]{5,2,3,1,4,0:T(8,128)(2,1)} %copy_dynamic-update-slice_fusion.18), kind=kOutput, calls=%fused_computation.71 | convolution fusion | flops 353894400 | bytes 5148672 | tf_op jit(solution)/shard_map/nhwtgc,tcgd->nhwgd/dot_general | solution.py:65
  259.1 3.1 %fusion.16 = bf16[1,1,5,40,1536]{4,3,2,1,0:T(8,128)(2,1)} fusion(f32[5,40,1536]{2,1,0:T(8,128)} %fusion.52, bf16[768,1536]{1,0:T(8,128)(2,1)S(1)} %copy-done, f32[5,40,768]{2,1,0:T(8,128)} %reshape.602), kind=kOutput, calls=%fused_computation.27 | convolution fusion | flops 474316800 | bytes 4816896 | tf_op jit(solution)/shard_map/dot_general | solution.py:31
  (108 shorter events, 37.5 us)
Async XLA Ops:
  0.0 259.1 %copy-start = (bf16[768,1536]{1,0:T(8,128)(2,1)S(1)}, bf16[768,1536]{1,0:T(8,128)(2,1)}, u32[]{:S(2)}) copy-start(bf16[768,1536]{1,0:T(8,128)(2,1)} %param.18) | copy-start | bytes 7077892
  0.0 4.8 %copy-start.16 = (bf16[512,256]{1,0:T(8,128)(2,1)S(1)}, bf16[512,256]{1,0:T(8,128)(2,1)}, u32[]{:S(2)}) copy-start(bf16[512,256]{1,0:T(8,128)(2,1)} %param.11) | copy-start | bytes 786436
  6.1 21.3 %copy-start.12 = (bf16[1152,256]{1,0:T(8,128)(2,1)S(1)}, bf16[1152,256]{1,0:T(8,128)(2,1)}, u32[]{:S(2)}) copy-start(bf16[1152,256]{1,0:T(8,128)(2,1)} %param.12) | copy-start | bytes 1769476
  10.5 5.5 %collective-permute-start = (bf16[1,8,1,10,256]{4,1,3,2,0:T(8,128)(2,1)S(1)}, bf16[1,8,1,10,256]{4,1,3,2,0:T(8,128)(2,1)S(1)}, u32[]{:S(2)}, u32[]{:S(2)}) collective-permute-start(bf16[1,8,1,10,256]{4,1,3,2,0:T(8,128)(2,1)S(1)} %get-tuple-element.40), channel_id=1, source_target_pairs={{0,8},{8,16},{16,24},{24,32},{32,40},{40,48},{48,56},{1,9},{9,17},... | collective-permute-start | bytes 122888 | tf_op jit(solution)/shard_map/ppermute | solution.py:17
  14.3 5.9 %collective-permute-start.1 = (bf16[1,8,1,10,256]{4,1,3,2,0:T(8,128)(2,1)S(1)}, bf16[1,8,1,10,256]{4,1,3,2,0:T(8,128)(2,1)S(1)}, u32[]{:S(2)}, u32[]{:S(2)}) collective-permute-start(bf16[1,8,1,10,256]{4,1,3,2,0:T(8,128)(2,1)S(1)} %get-tuple-element.41), channel_id=1, source_target_pairs={{8,0},{16,8},{24,16},{32,24},{40,32},{48,40},{56,48},{9,1},{17,9},... | collective-permute-start | bytes 122888 | tf_op jit(solution)/shard_map/ppermute | solution.py:20
  20.9 7.5 %collective-permute-start.2 = (bf16[1,8,12,1,256]{4,1,3,2,0:T(8,128)(2,1)}, bf16[1,8,12,1,256]{4,1,3,2,0:T(8,128)(2,1)S(1)}, u32[]{:S(2)}, u32[]{:S(2)}) collective-permute-start(bf16[1,8,12,1,256]{4,1,3,2,0:T(8,128)(2,1)} %get-tuple-element.36), channel_id=1, source_target_pairs={{0,1},{1,2},{2,3},{3,4},{4,5},{5,6},{6,7},{8,9},{9,10},{10,11},{11... | collective-permute-start | bytes 147464 | tf_op jit(solution)/shard_map/ppermute | solution.py:17
  25.5 9.8 %collective-permute-start.3 = (bf16[1,8,12,1,256]{4,1,3,2,0:T(8,128)(2,1)}, bf16[1,8,12,1,256]{4,1,3,2,0:T(8,128)(2,1)S(1)}, u32[]{:S(2)}, u32[]{:S(2)}) collective-permute-start(bf16[1,8,12,1,256]{4,1,3,2,0:T(8,128)(2,1)} %get-tuple-element.37), channel_id=1, source_target_pairs={{1,0},{2,1},{3,2},{4,3},{5,4},{6,5},{7,6},{9,8},{10,9},{11,10},{12... | collective-permute-start | bytes 147464 | tf_op jit(solution)/shard_map/ppermute | solution.py:20
  36.7 1.1 copy-start.14
  39.4 18.1 %copy-start.13 = (bf16[1152,256]{1,0:T(8,128)(2,1)S(1)}, bf16[1152,256]{1,0:T(8,128)(2,1)}, u32[]{:S(2)}) copy-start(bf16[1152,256]{1,0:T(8,128)(2,1)} %param.13) | copy-start | bytes 1769476
  40.1 5.5 %collective-permute-start.4 = (bf16[1,8,1,10,256]{4,1,3,2,0:T(8,128)(2,1)S(1)}, bf16[1,8,1,10,256]{4,1,3,2,0:T(8,128)(2,1)S(1)}, u32[]{:S(2)}, u32[]{:S(2)}) collective-permute-start(bf16[1,8,1,10,256]{4,1,3,2,0:T(8,128)(2,1)S(1)} %get-tuple-element.38), channel_id=1, source_target_pairs={{0,8},{8,16},{16,24},{24,32},{32,40},{40,48},{48,56},{1,9},{9,17},... | collective-permute-start | bytes 122888 | tf_op jit(solution)/shard_map/ppermute | solution.py:17
  43.9 6.9 %collective-permute-start.5 = (bf16[1,8,1,10,256]{4,1,3,2,0:T(8,128)(2,1)S(1)}, bf16[1,8,1,10,256]{4,1,3,2,0:T(8,128)(2,1)S(1)}, u32[]{:S(2)}, u32[]{:S(2)}) collective-permute-start(bf16[1,8,1,10,256]{4,1,3,2,0:T(8,128)(2,1)S(1)} %get-tuple-element.39), channel_id=1, source_target_pairs={{8,0},{16,8},{24,16},{32,24},{40,32},{48,40},{56,48},{9,1},{17,9},... | collective-permute-start | bytes 122888 | tf_op jit(solution)/shard_map/ppermute | solution.py:20
  51.5 7.0 %collective-permute-start.6 = (bf16[1,8,12,1,256]{4,1,3,2,0:T(8,128)(2,1)}, bf16[1,8,12,1,256]{4,1,3,2,0:T(8,128)(2,1)S(1)}, u32[]{:S(2)}, u32[]{:S(2)}) collective-permute-start(bf16[1,8,12,1,256]{4,1,3,2,0:T(8,128)(2,1)} %get-tuple-element.34), channel_id=1, source_target_pairs={{0,1},{1,2},{2,3},{3,4},{4,5},{5,6},{6,7},{8,9},{9,10},{10,11},{11... | collective-permute-start | bytes 147464 | tf_op jit(solution)/shard_map/ppermute | solution.py:17
  53.4 9.8 %collective-permute-start.7 = (bf16[1,8,12,1,256]{4,1,3,2,0:T(8,128)(2,1)}, bf16[1,8,12,1,256]{4,1,3,2,0:T(8,128)(2,1)S(1)}, u32[]{:S(2)}, u32[]{:S(2)}) collective-permute-start(bf16[1,8,12,1,256]{4,1,3,2,0:T(8,128)(2,1)} %get-tuple-element.35), channel_id=1, source_target_pairs={{1,0},{2,1},{3,2},{4,3},{5,4},{6,5},{7,6},{9,8},{10,9},{11,10},{12... | collective-permute-start | bytes 147464 | tf_op jit(solution)/shard_map/ppermute | solution.py:20
  64.6 1.1 copy-start.15
  65.7 1.7 copy-start.11
  65.7 1.7 copy-start.18
  104.2 16.4 %all-to-all-start.1 = ((bf16[1,1,80,10,512]{4,3,1,0,2:T(8,128)(2,1)}), bf16[1,1,80,10,512]{4,3,1,0,2:T(8,128)(2,1)}, u32[]{:S(2)}, u32[]{:S(2)}) async-start(bf16[1,1,80,10,512]{4,3,1,0,2:T(8,128)(2,1)} %bitcast.160), calls=%async_computation.1 | async-start | bytes 2621440 | tf_op jit(solution)/shard_map/all_to_all | solution.py:79
  125.0 3.4 %copy-start.1 = (f32[1,1,8,10,10,512]{5,1,4,3,2,0:T(1,128)S(1)}, f32[1,1,8,10,10,512]{5,1,4,3,2,0:T(1,128)}, u32[]{:S(2)}) copy-start(f32[1,1,8,10,10,512]{5,1,4,3,2,0:T(1,128)} %reshape.605) | copy-start | bytes 4915204
  131.1 2.8 %copy-start.17 = (bf16[512,768]{1,0:T(8,128)(2,1)S(1)}, bf16[512,768]{1,0:T(8,128)(2,1)}, u32[]{:S(2)}) copy-start(bf16[512,768]{1,0:T(8,128)(2,1)} %param.15) | copy-start | bytes 2359300
  136.4 7.6 %copy-start.4 = (f32[1,1,10,8,10,512]{5,1,4,3,2,0:T(1,128)S(1)}, f32[1,1,10,8,10,512]{5,1,4,3,2,0:T(1,128)}, u32[]{:S(2)}) copy-start(f32[1,1,10,8,10,512]{5,1,4,3,2,0:T(1,128)} %copy.262) | copy-start | bytes 4915204
  137.3 8.2 %collective-permute-start.8 = (bf16[1,1,1,80,768]{4,3,2,1,0:T(8,128)(2,1)S(1)}, bf16[1,1,1,80,768]{4,3,2,1,0:T(8,128)(2,1)S(1)}, u32[]{:S(2)}, u32[]{:S(2)}) collective-permute-start(bf16[1,1,1,80,768]{4,3,2,1,0:T(8,128)(2,1)S(1)} %get-tuple-element.5), channel_id=1, source_target_pairs={{0,1},{1,2},{2,3},{3,4},{4,5},{5,6},{6,7},{8,9},{9,10},{10,11},{11... | collective-permute-start | bytes 368648 | tf_op jit(solution)/shard_map/ppermute | solution.py:17
  141.9 10.4 %collective-permute-start.9 = (bf16[1,1,1,80,768]{4,3,2,1,0:T(8,128)(2,1)S(1)}, bf16[1,1,1,80,768]{4,3,2,1,0:T(8,128)(2,1)S(1)}, u32[]{:S(2)}, u32[]{:S(2)}) collective-permute-start(bf16[1,1,1,80,768]{4,3,2,1,0:T(8,128)(2,1)S(1)} %get-tuple-element.6), channel_id=1, source_target_pairs={{1,0},{2,1},{3,2},{4,3},{5,4},{6,5},{7,6},{9,8},{10,9},{11,10},{12... | collective-permute-start | bytes 368648 | tf_op jit(solution)/shard_map/ppermute | solution.py:20
  188.5 11.6 %copy-start.9 = (bf16[1,5,40,768]{3,2,1,0:T(8,128)(2,1)S(1)}, bf16[1,5,40,768]{3,2,1,0:T(8,128)(2,1)}, u32[]{:S(2)}) copy-start(bf16[1,5,40,768]{3,2,1,0:T(8,128)(2,1)} %slice.179) | copy-start | bytes 921604
  200.9 7.4 %copy-start.8 = (bf16[1,5,40,1,6,128]{5,4,2,1,3,0:T(8,128)(2,1)S(1)}, bf16[1,5,40,1,6,128]{5,4,2,1,3,0:T(8,128)(2,1)}, u32[]{:S(2)}) copy-start(bf16[1,5,40,1,6,128]{5,4,2,1,3,0:T(8,128)(2,1)} %stack.145) | copy-start | bytes 921604
  200.9 8.2 %copy-start.6 = (bf16[1,5,40,1,6,128]{5,4,2,1,3,0:T(8,128)(2,1)S(1)}, bf16[1,5,40,1,6,128]{5,4,2,1,3,0:T(8,128)(2,1)}, u32[]{:S(2)}) copy-start(bf16[1,5,40,1,6,128]{5,4,2,1,3,0:T(8,128)(2,1)} %stack.146) | copy-start | bytes 921604
  202.8 8.7 %copy-start.3 = (bf16[9,128,6,128]{3,2,1,0:T(8,128)(2,1)S(1)}, bf16[9,128,6,128]{3,2,1,0:T(8,128)(2,1)}, u32[]{:S(2)}) copy-start(bf16[9,128,6,128]{3,2,1,0:T(8,128)(2,1)} %reshape.597) | copy-start | bytes 5308420
  216.8 9.3 %collective-permute-start.10 = (bf16[1,1,1,40,768]{4,3,2,1,0:T(8,128)(2,1)S(1)}, bf16[1,1,1,40,768]{4,3,2,1,0:T(8,128)(2,1)S(1)}, u32[]{:S(2)}, u32[]{:S(2)}) collective-permute-start(bf16[1,1,1,40,768]{4,3,2,1,0:T(8,128)(2,1)S(1)} %get-tuple-element.42), channel_id=1, source_target_pairs={{0,1},{1,2},{2,3},{3,4},{4,5},{5,6},{6,7},{8,9},{9,10},{10,11},{11... | collective-permute-start | bytes 184328 | tf_op jit(solution)/shard_map/ppermute | solution.py:17
  218.7 9.7 %collective-permute-start.11 = (bf16[1,1,1,40,768]{4,3,2,1,0:T(8,128)(2,1)S(1)}, bf16[1,1,1,40,768]{4,3,2,1,0:T(8,128)(2,1)S(1)}, u32[]{:S(2)}, u32[]{:S(2)}) collective-permute-start(bf16[1,1,1,40,768]{4,3,2,1,0:T(8,128)(2,1)S(1)} %get-tuple-element.43), channel_id=1, source_target_pairs={{1,0},{2,1},{3,2},{4,3},{5,4},{6,5},{7,6},{9,8},{10,9},{11,10},{12... | collective-permute-start | bytes 184328 | tf_op jit(solution)/shard_map/ppermute | solution.py:20
  232.1 10.5 %copy-start.10 = (bf16[1,5,40,768]{3,2,1,0:T(8,128)(2,1)S(1)}, bf16[1,5,40,768]{3,2,1,0:T(8,128)(2,1)}, u32[]{:S(2)}) copy-start(bf16[1,5,40,768]{3,2,1,0:T(8,128)(2,1)} %get-tuple-element.27) | copy-start | bytes 921604
  244.5 7.4 %copy-start.7 = (bf16[1,5,40,1,6,128]{5,4,2,1,3,0:T(8,128)(2,1)S(1)}, bf16[1,5,40,1,6,128]{5,4,2,1,3,0:T(8,128)(2,1)}, u32[]{:S(2)}) copy-start(bf16[1,5,40,1,6,128]{5,4,2,1,3,0:T(8,128)(2,1)} %stack.155) | copy-start | bytes 921604
  244.5 8.2 %copy-start.5 = (bf16[1,5,40,1,6,128]{5,4,2,1,3,0:T(8,128)(2,1)S(1)}, bf16[1,5,40,1,6,128]{5,4,2,1,3,0:T(8,128)(2,1)}, u32[]{:S(2)}) copy-start(bf16[1,5,40,1,6,128]{5,4,2,1,3,0:T(8,128)(2,1)} %stack.156) | copy-start | bytes 921604
  246.3 8.7 %copy-start.2 = (bf16[9,128,6,128]{3,2,1,0:T(8,128)(2,1)S(1)}, bf16[9,128,6,128]{3,2,1,0:T(8,128)(2,1)}, u32[]{:S(2)}) copy-start(bf16[9,128,6,128]{3,2,1,0:T(8,128)(2,1)} %reshape.601) | copy-start | bytes 5308420
where the time goes:
time: 264 us; the launch traced here: 262 us
  local copies, waits for them, and re-layouts  121 us (46%)
  starting transfers between devices  40.1 us (15%)
  blocking collectives  35.7 us (14%)
  waiting for transfers between devices  33.6 us (13%)
  matrix products  19.9 us (8%)
  other arithmetic  11.4 us (4%)
    all_to_all x1, blocking collectives, relayout(): lax.all_to_all(tensor, 'row', split_axis=1, concat_axis=2, tiled=True)  35.7 us
    slice x10, local copies, waits for them, and re-layouts, group_conv(): lax.slice(merged, (0, start_row, start_col, 0), (batches, start_row + str...  33.9 us
    another operation x24, local copies, waits for them, and re-layouts, group_conv(): stacked = jnp.stack(tap_list, axis=3)  30.4 us
    ppermute x6, waiting for transfers between devices, with_halo(): lax.ppermute(lax.slice_in_dim(block, 0, width, axis=dim), axis, backward)  30.3 us
    unnamed x70, local copies, waits for them, and re-layouts  24.3 us
    ppermute x6, starting transfers between devices, with_halo(): lax.ppermute(lax.slice_in_dim(block, block.shape[dim] - width, None, axis...  20.6 us
    ppermute x6, starting transfers between devices, with_halo(): lax.ppermute(lax.slice_in_dim(block, 0, width, axis=dim), axis, backward)  15 us
    convert_element_type x4, local copies, waits for them, and re-layouts, transition(): block_result.astype(jnp.float32)  13.2 us
  transfers between devices with their start and end apart: 13, of which 9 were waited for; matrix products, arithmetic and copies ran while one was open for 6% of the time, Pallas kernels for 0%

commit v1 on v0

--- a/solution.py
+++ b/solution.py
@@ -76,12 +76,20 @@
 
 
 def relayout(tensor):
-    return lax.all_to_all(
-        lax.all_to_all(tensor, "row", split_axis=1, concat_axis=2, tiled=True),
-        "col",
-        split_axis=2,
-        concat_axis=3,
-        tiled=True,
+    return jnp.concatenate(
+        lax.all_to_all(
+            jnp.stack(
+                jnp.split(
+                    lax.all_to_all(tensor, "row", split_axis=1, concat_axis=2, tiled=True),
+                    lax.axis_size("col"),
+                    axis=2,
+                )
+            ),
+            "col",
+            0,
+            0,
+        ),
+        axis=3,
     )
 
 

time: 264 us -> 266 us (level)
    convert_element_type x4 -> x3, local copies, waits for them, and re-layouts: 13.2 us -> 7.53 us  [transition(): block_result.astype(jnp.float32)]
    unnamed x70 -> x75, local copies, waits for them, and re-layouts: 24.3 us -> 29.3 us
where the time goes in v1:
time: 266 us; the launch traced here: 264 us
  local copies, waits for them, and re-layouts  121 us (45%)
  starting transfers between devices  40.1 us (15%)
  blocking collectives  35.6 us (13%)
  waiting for transfers between devices  33.6 us (13%)
  matrix products  19.9 us (7%)
  other arithmetic  13.1 us (5%)
    all_to_all x1, blocking collectives, relayout(): lax.all_to_all(tensor, 'row', split_axis=1, concat_axis=2, tiled=True)  35.6 us
    slice x10, local copies, waits for them, and re-layouts, group_conv(): lax.slice(merged, (0, start_row, start_col, 0), (batches, start_row + str...  33.9 us
    ppermute x6, waiting for transfers between devices, with_halo(): lax.ppermute(lax.slice_in_dim(block, 0, width, axis=dim), axis, backward)  30.3 us
    another operation x24, local copies, waits for them, and re-layouts, group_conv(): stacked = jnp.stack(tap_list, axis=3)  30.3 us
    unnamed x75, local copies, waits for them, and re-layouts  29.3 us
    ppermute x6, starting transfers between devices, with_halo(): lax.ppermute(lax.slice_in_dim(block, block.shape[dim] - width, None, axis...  20.6 us
    ppermute x6, starting transfers between devices, with_halo(): lax.ppermute(lax.slice_in_dim(block, 0, width, axis=dim), axis, backward)  15 us
    reshape x4, local copies, waits for them, and re-layouts, group_conv(): kernel = weight.reshape(9, group_width, groups, group_width)  11.2 us
  transfers between devices with their start and end apart: 13, of which 9 were waited for; matrix products, arithmetic and copies ran while one was open for 6% of the time, Pallas kernels for 0%

profile of v1, /device:TPU:24, one launch (start us, length us, event | category | flops | bytes accessed | tf_op | source)
XLA Modules:
  0.0 263.6 jit_solution(1081888083087245933)
XLA Ops:
  0.0 1.9 fusion.47
  3.3 1.4 reshape.584
  6.1 2.4 reshape.585
  8.5 2.0 fusion.73
  10.5 3.8 %collective-permute-start = (bf16[1,8,1,10,256]{4,1,3,2,0:T(8,128)(2,1)S(1)}, bf16[1,8,1,10,256]{4,1,3,2,0:T(8,128)(2,1)S(1)}, u32[]{:S(2)}, u32[]{:S(2)}) collective-permute-start(bf16[1,8,1,10,256]{4,1,3,2,0:T(8,128)(2,1)S(1)} %get-tuple-element.40), channel_id=1, source_target_pairs={{0,8},{8,16},{16,24},{24,32},{32,40},{40,48},{48,56},{1,9},{9,17},... | collective-permute-start | bytes 122888 | tf_op jit(solution)/shard_map/ppermute | solution.py:17
  16.0 4.2 %collective-permute-done.1 = bf16[1,8,1,10,256]{4,1,3,2,0:T(8,128)(2,1)S(1)} collective-permute-done((bf16[1,8,1,10,256]{4,1,3,2,0:T(8,128)(2,1)S(1)}, bf16[1,8,1,10,256]{4,1,3,2,0:T(8,128)(2,1)S(1)}, u32[]{:S(2)}, u32[]{:S(2)}) %collective-permute-start.1) | collective-permute-done | bytes 40992 | tf_op jit(solution)/shard_map/ppermute | solution.py:20
  20.8 4.6 %collective-permute-start.2 = (bf16[1,8,12,1,256]{4,1,3,2,0:T(8,128)(2,1)}, bf16[1,8,12,1,256]{4,1,3,2,0:T(8,128)(2,1)S(1)}, u32[]{:S(2)}, u32[]{:S(2)}) collective-permute-start(bf16[1,8,12,1,256]{4,1,3,2,0:T(8,128)(2,1)} %get-tuple-element.36), channel_id=1, source_target_pairs={{0,1},{1,2},{2,3},{3,4},{4,5},{5,6},{6,7},{8,9},{9,10},{10,11},{11... | collective-permute-start | bytes 147464 | tf_op jit(solution)/shard_map/ppermute | solution.py:17
  25.4 1.9 collective-permute-start.3
  28.3 6.9 %collective-permute-done.3 = bf16[1,8,12,1,256]{4,1,3,2,0:T(8,128)(2,1)S(1)} collective-permute-done((bf16[1,8,12,1,256]{4,1,3,2,0:T(8,128)(2,1)}, bf16[1,8,12,1,256]{4,1,3,2,0:T(8,128)(2,1)S(1)}, u32[]{:S(2)}, u32[]{:S(2)}) %collective-permute-start.3) | collective-permute-done | bytes 49184 | tf_op jit(solution)/shard_map/ppermute | solution.py:20
  37.7 1.7 convolution_bitcast_fusion.1
  40.0 3.8 %collective-permute-start.4 = (bf16[1,8,1,10,256]{4,1,3,2,0:T(8,128)(2,1)S(1)}, bf16[1,8,1,10,256]{4,1,3,2,0:T(8,128)(2,1)S(1)}, u32[]{:S(2)}, u32[]{:S(2)}) collective-permute-start(bf16[1,8,1,10,256]{4,1,3,2,0:T(8,128)(2,1)S(1)} %get-tuple-element.38), channel_id=1, source_target_pairs={{0,8},{8,16},{16,24},{24,32},{32,40},{40,48},{48,56},{1,9},{9,17},... | collective-permute-start | bytes 122888 | tf_op jit(solution)/shard_map/ppermute | solution.py:17
  45.5 5.3 %collective-permute-done.5 = bf16[1,8,1,10,256]{4,1,3,2,0:T(8,128)(2,1)S(1)} collective-permute-done((bf16[1,8,1,10,256]{4,1,3,2,0:T(8,128)(2,1)S(1)}, bf16[1,8,1,10,256]{4,1,3,2,0:T(8,128)(2,1)S(1)}, u32[]{:S(2)}, u32[]{:S(2)}) %collective-permute-start.5) | collective-permute-done | bytes 40992 | tf_op jit(solution)/shard_map/ppermute | solution.py:20
  51.4 1.9 collective-permute-start.6
  53.4 4.1 %collective-permute-start.7 = (bf16[1,8,12,1,256]{4,1,3,2,0:T(8,128)(2,1)}, bf16[1,8,12,1,256]{4,1,3,2,0:T(8,128)(2,1)S(1)}, u32[]{:S(2)}, u32[]{:S(2)}) collective-permute-start(bf16[1,8,12,1,256]{4,1,3,2,0:T(8,128)(2,1)} %get-tuple-element.35), channel_id=1, source_target_pairs={{1,0},{2,1},{3,2},{4,3},{5,4},{6,5},{7,6},{9,8},{10,9},{11,10},{12... | collective-permute-start | bytes 147464 | tf_op jit(solution)/shard_map/ppermute | solution.py:20
  58.4 4.7 %collective-permute-done.7 = bf16[1,8,12,1,256]{4,1,3,2,0:T(8,128)(2,1)S(1)} collective-permute-done((bf16[1,8,12,1,256]{4,1,3,2,0:T(8,128)(2,1)}, bf16[1,8,12,1,256]{4,1,3,2,0:T(8,128)(2,1)S(1)}, u32[]{:S(2)}, u32[]{:S(2)}) %collective-permute-start.7) | collective-permute-done | bytes 49184 | tf_op jit(solution)/shard_map/ppermute | solution.py:20
  65.6 1.7 convolution_bitcast_fusion
  68.5 35.6 %all_to_all.17 = bf16[1,8,10,10,512]{4,3,2,0,1:T(8,128)(2,1)S(1)} all-to-all(bf16[1,8,10,10,512]{4,3,2,0,1:T(8,128)(2,1)S(1)} %copy.194), channel_id=1, replica_groups=mesh['section'=4,'row'=8,'col'=8] {'row'}, dimensions={1} | all-to-all | bytes 1638400 | tf_op jit(solution)/shard_map/all_to_all | solution.py:83
  109.5 4.5 %all-to-all-start.1 = ((bf16[8,1,1,10,10,512]{5,4,3,2,1,0:T(8,128)(2,1)}), bf16[8,1,1,10,10,512]{5,4,3,2,1,0:T(8,128)(2,1)}, u32[]{:S(2)}, u32[]{:S(2)}) async-start(bf16[8,1,1,10,10,512]{5,4,3,2,1,0:T(8,128)(2,1)} %fusion.139), calls=%async_computation.1 | async-start | bytes 2621440 | tf_op jit(solution)/shard_map/all_to_all | solution.py:80
  114.1 4.7 %reshape.595 = bf16[9,128,6,128]{3,2,1,0:T(8,128)(2,1)} reshape(bf16[1152,768]{1,0:T(8,128)(2,1)} %param.16) | data formatting | bytes 3538944 | tf_op jit(solution)/shard_map/reshape | solution.py:64
  118.7 4.7 %reshape.599 = bf16[9,128,6,128]{3,2,1,0:T(8,128)(2,1)} reshape(bf16[1152,768]{1,0:T(8,128)(2,1)} %param.17) | data formatting | bytes 3538944 | tf_op jit(solution)/shard_map/reshape | solution.py:64
  123.4 2.6 all-to-all-done.1
  125.9 1.7 convert_bitcast_fusion
  127.6 1.8 copy.201
  129.4 2.9 %copy.195 = f32[1,1,10,8,10,512]{5,1,4,3,2,0:T(1,128)} copy(f32[1,1,10,8,10,512]{5,4,2,1,0,3:T(8,128)S(1)} %convert_bitcast_fusion) | data formatting | bytes 3276800 | tf_op jit(solution)/shard_map/convert_element_type | solution.py:99
  132.4 2.8 %reshape.602 = f32[800,512]{1,0:T(8,128)} reshape(f32[1,1,10,8,10,512]{5,4,3,2,1,0:T(8,128)} %copy.201) | data formatting | bytes 3276800 | tf_op jit(solution)/shard_map/convert_element_type | solution.py:99
  135.2 2.6 fusion.92
  138.6 4.5 %collective-permute-start.8 = (bf16[1,1,1,80,768]{4,3,2,1,0:T(8,128)(2,1)S(1)}, bf16[1,1,1,80,768]{4,3,2,1,0:T(8,128)(2,1)S(1)}, u32[]{:S(2)}, u32[]{:S(2)}) collective-permute-start(bf16[1,1,1,80,768]{4,3,2,1,0:T(8,128)(2,1)S(1)} %get-tuple-element.5), channel_id=1, source_target_pairs={{0,1},{1,2},{2,3},{3,4},{4,5},{5,6},{6,7},{8,9},{9,10},{10,11},{11... | collective-permute-start | bytes 368648 | tf_op jit(solution)/shard_map/ppermute | solution.py:17
  143.2 2.2 collective-permute-start.9
  146.8 6.8 %collective-permute-done.9 = bf16[1,1,1,80,768]{4,3,2,1,0:T(8,128)(2,1)S(1)} collective-permute-done((bf16[1,1,1,80,768]{4,3,2,1,0:T(8,128)(2,1)S(1)}, bf16[1,1,1,80,768]{4,3,2,1,0:T(8,128)(2,1)S(1)}, u32[]{:S(2)}, u32[]{:S(2)}) %collective-permute-start.9) | collective-permute-done | bytes 122912 | tf_op jit(solution)/shard_map/ppermute | solution.py:20
  153.6 1.6 fusion.51
  155.2 3.7 %slice.172 = bf16[1,5,40,768]{3,2,1,0:T(8,128)(2,1)} slice(bf16[1,12,82,768]{3,2,1,0:T(8,128)(2,1)} %fusion.51), slice={[0:1:1], [1:10:2], [1:80:2], [0:768:1]} | slice | bytes 614400 | tf_op jit(solution)/shard_map/slice | solution.py:49
  158.9 3.8 %slice.173 = bf16[1,5,40,768]{3,2,1,0:T(8,128)(2,1)} slice(bf16[1,12,82,768]{3,2,1,0:T(8,128)(2,1)} %fusion.51), slice={[0:1:1], [1:10:2], [2:81:2], [0:768:1]} | slice | bytes 614400 | tf_op jit(solution)/shard_map/slice | solution.py:49
  162.7 3.8 %slice.174 = bf16[1,5,40,768]{3,2,1,0:T(8,128)(2,1)} slice(bf16[1,12,82,768]{3,2,1,0:T(8,128)(2,1)} %fusion.51), slice={[0:1:1], [1:10:2], [3:82:2], [0:768:1]} | slice | bytes 614400 | tf_op jit(solution)/shard_map/slice | solution.py:49
  166.5 3.8 %slice.175 = bf16[1,5,40,768]{3,2,1,0:T(8,128)(2,1)} slice(bf16[1,12,82,768]{3,2,1,0:T(8,128)(2,1)} %fusion.51), slice={[0:1:1], [2:11:2], [1:80:2], [0:768:1]} | slice | bytes 614400 | tf_op jit(solution)/shard_map/slice | solution.py:49
  170.3 3.8 %slice.176 = bf16[1,5,40,768]{3,2,1,0:T(8,128)(2,1)} slice(bf16[1,12,82,768]{3,2,1,0:T(8,128)(2,1)} %fusion.51), slice={[0:1:1], [2:11:2], [2:81:2], [0:768:1]} | slice | bytes 614400 | tf_op jit(solution)/shard_map/slice | solution.py:49
  174.1 3.8 %slice.177 = bf16[1,5,40,768]{3,2,1,0:T(8,128)(2,1)} slice(bf16[1,12,82,768]{3,2,1,0:T(8,128)(2,1)} %fusion.51), slice={[0:1:1], [2:11:2], [3:82:2], [0:768:1]} | slice | bytes 614400 | tf_op jit(solution)/shard_map/slice | solution.py:49
  177.8 3.0 %slice.178 = bf16[1,5,40,768]{3,2,1,0:T(8,128)(2,1)S(1)} slice(bf16[1,12,82,768]{3,2,1,0:T(8,128)(2,1)} %fusion.51), slice={[0:1:1], [3:12:2], [1:80:2], [0:768:1]} | slice | bytes 614400 | tf_op jit(solution)/shard_map/slice | solution.py:49
  180.9 3.8 %slice.179 = bf16[1,5,40,768]{3,2,1,0:T(8,128)(2,1)} slice(bf16[1,12,82,768]{3,2,1,0:T(8,128)(2,1)} %fusion.51), slice={[0:1:1], [3:12:2], [2:81:2], [0:768:1]} | slice | bytes 614400 | tf_op jit(solution)/shard_map/slice | solution.py:49
  184.6 3.1 %slice.180 = bf16[1,5,40,768]{3,2,1,0:T(8,128)(2,1)S(1)} slice(bf16[1,12,82,768]{3,2,1,0:T(8,128)(2,1)} %fusion.51), slice={[0:1:1], [3:12:2], [3:82:2], [0:768:1]} | slice | bytes 614400 | tf_op jit(solution)/shard_map/slice | solution.py:49
  189.8 2.1 stack.177
  191.9 2.1 stack.178
  194.0 2.1 stack.179
  196.1 2.1 stack.180
  198.2 2.1 stack.181
  202.2 1.9 copy_dynamic-update-slice_fusion.34
  204.1 1.9 copy_dynamic-update-slice_fusion.33
  206.0 1.8 copy_dynamic-update-slice_fusion.32
  207.8 1.8 copy_dynamic-update-slice_fusion.31
  212.8 2.9 %fusion.54 = f32[1,5,40,6,128]{4,2,1,3,0:T(8,128)S(1)} fusion(bf16[9,128,6,128,1]{3,2,1,0,4:T(8,128)(2,1)S(1)} %bitcast.185, bf16[1,5,40,9,6,128]{5,2,3,1,4,0:T(8,128)(2,1)} %copy_dynamic-update-slice_fusion.27), kind=kOutput, calls=%fused_computation.71 | convolution fusion | flops 353894400 | bytes 5148672 | tf_op jit(solution)/shard_map/nhwtgc,tcgd->nhwgd/dot_general | solution.py:65
  218.1 1.9 collective-permute-start.10
  220.0 4.2 %collective-permute-start.11 = (bf16[1,1,1,40,768]{4,3,2,1,0:T(8,128)(2,1)S(1)}, bf16[1,1,1,40,768]{4,3,2,1,0:T(8,128)(2,1)S(1)}, u32[]{:S(2)}, u32[]{:S(2)}) collective-permute-start(bf16[1,1,1,40,768]{4,3,2,1,0:T(8,128)(2,1)S(1)} %get-tuple-element.43), channel_id=1, source_target_pairs={{1,0},{2,1},{3,2},{4,3},{5,4},{6,5},{7,6},{9,8},{10,9},{11,10},{12... | collective-permute-start | bytes 184328 | tf_op jit(solution)/shard_map/ppermute | solution.py:20
  224.3 3.1 %fusion.52 = f32[5,40,1536]{2,1,0:T(8,128)} fusion(bf16[512,1536]{1,0:T(8,128)(2,1)} %param.19, f32[5,40,512]{2,1,0:T(8,128)} %convert_reduce_fusion), kind=kOutput, calls=%fused_computation.65 | convolution fusion | flops 314777600 | bytes 3211264 | tf_op jit(solution)/shard_map/dot_general | solution.py:31
  227.3 2.4 collective-permute-done.11
  233.5 2.1 stack.187
  235.6 2.1 stack.188
  237.7 2.1 stack.189
  239.8 2.1 stack.190
  241.9 2.1 stack.191
  245.8 1.9 copy_dynamic-update-slice_fusion.25
  247.7 2.0 copy_dynamic-update-slice_fusion.24
  249.7 1.8 copy_dynamic-update-slice_fusion.23
  251.5 1.8 copy_dynamic-update-slice_fusion.22
  256.5 2.9 %fusion.59 = f32[1,5,40,6,128]{4,2,1,3,0:T(8,128)S(1)} fusion(bf16[9,128,6,128,1]{3,2,1,0,4:T(8,128)(2,1)S(1)} %bitcast.184, bf16[1,5,40,9,6,128]{5,2,3,1,4,0:T(8,128)(2,1)} %copy_dynamic-update-slice_fusion.18), kind=kOutput, calls=%fused_computation.72 | convolution fusion | flops 353894400 | bytes 5148672 | tf_op jit(solution)/shard_map/nhwtgc,tcgd->nhwgd/dot_general | solution.py:65
  260.5 3.1 %fusion.16 = bf16[1,1,5,40,1536]{4,3,2,1,0:T(8,128)(2,1)} fusion(f32[5,40,1536]{2,1,0:T(8,128)} %fusion.52, bf16[768,1536]{1,0:T(8,128)(2,1)S(1)} %copy-done, f32[5,40,768]{2,1,0:T(8,128)} %reshape.600), kind=kOutput, calls=%fused_computation.28 | convolution fusion | flops 474316800 | bytes 4816896 | tf_op jit(solution)/shard_map/dot_general | solution.py:31
  (114 shorter events, 42.9 us)
Async XLA Ops:
  0.0 260.5 %copy-start = (bf16[768,1536]{1,0:T(8,128)(2,1)S(1)}, bf16[768,1536]{1,0:T(8,128)(2,1)}, u32[]{:S(2)}) copy-start(bf16[768,1536]{1,0:T(8,128)(2,1)} %param.18) | copy-start | bytes 7077892
  1.9 2.9 %copy-start.15 = (bf16[512,256]{1,0:T(8,128)(2,1)S(1)}, bf16[512,256]{1,0:T(8,128)(2,1)}, u32[]{:S(2)}) copy-start(bf16[512,256]{1,0:T(8,128)(2,1)} %param.11) | copy-start | bytes 786436
  6.1 21.3 %copy-start.11 = (bf16[1152,256]{1,0:T(8,128)(2,1)S(1)}, bf16[1152,256]{1,0:T(8,128)(2,1)}, u32[]{:S(2)}) copy-start(bf16[1152,256]{1,0:T(8,128)(2,1)} %param.12) | copy-start | bytes 1769476
  10.5 5.5 %collective-permute-start = (bf16[1,8,1,10,256]{4,1,3,2,0:T(8,128)(2,1)S(1)}, bf16[1,8,1,10,256]{4,1,3,2,0:T(8,128)(2,1)S(1)}, u32[]{:S(2)}, u32[]{:S(2)}) collective-permute-start(bf16[1,8,1,10,256]{4,1,3,2,0:T(8,128)(2,1)S(1)} %get-tuple-element.40), channel_id=1, source_target_pairs={{0,8},{8,16},{16,24},{24,32},{32,40},{40,48},{48,56},{1,9},{9,17},... | collective-permute-start | bytes 122888 | tf_op jit(solution)/shard_map/ppermute | solution.py:17
  14.3 5.9 %collective-permute-start.1 = (bf16[1,8,1,10,256]{4,1,3,2,0:T(8,128)(2,1)S(1)}, bf16[1,8,1,10,256]{4,1,3,2,0:T(8,128)(2,1)S(1)}, u32[]{:S(2)}, u32[]{:S(2)}) collective-permute-start(bf16[1,8,1,10,256]{4,1,3,2,0:T(8,128)(2,1)S(1)} %get-tuple-element.41), channel_id=1, source_target_pairs={{8,0},{16,8},{24,16},{32,24},{40,32},{48,40},{56,48},{9,1},{17,9},... | collective-permute-start | bytes 122888 | tf_op jit(solution)/shard_map/ppermute | solution.py:20
  20.8 7.5 %collective-permute-start.2 = (bf16[1,8,12,1,256]{4,1,3,2,0:T(8,128)(2,1)}, bf16[1,8,12,1,256]{4,1,3,2,0:T(8,128)(2,1)S(1)}, u32[]{:S(2)}, u32[]{:S(2)}) collective-permute-start(bf16[1,8,12,1,256]{4,1,3,2,0:T(8,128)(2,1)} %get-tuple-element.36), channel_id=1, source_target_pairs={{0,1},{1,2},{2,3},{3,4},{4,5},{5,6},{6,7},{8,9},{9,10},{10,11},{11... | collective-permute-start | bytes 147464 | tf_op jit(solution)/shard_map/ppermute | solution.py:17
  25.4 9.8 %collective-permute-start.3 = (bf16[1,8,12,1,256]{4,1,3,2,0:T(8,128)(2,1)}, bf16[1,8,12,1,256]{4,1,3,2,0:T(8,128)(2,1)S(1)}, u32[]{:S(2)}, u32[]{:S(2)}) collective-permute-start(bf16[1,8,12,1,256]{4,1,3,2,0:T(8,128)(2,1)} %get-tuple-element.37), channel_id=1, source_target_pairs={{1,0},{2,1},{3,2},{4,3},{5,4},{6,5},{7,6},{9,8},{10,9},{11,10},{12... | collective-permute-start | bytes 147464 | tf_op jit(solution)/shard_map/ppermute | solution.py:20
  36.6 1.1 copy-start.13
  39.4 18.1 %copy-start.12 = (bf16[1152,256]{1,0:T(8,128)(2,1)S(1)}, bf16[1152,256]{1,0:T(8,128)(2,1)}, u32[]{:S(2)}) copy-start(bf16[1152,256]{1,0:T(8,128)(2,1)} %param.13) | copy-start | bytes 1769476
  40.0 5.5 %collective-permute-start.4 = (bf16[1,8,1,10,256]{4,1,3,2,0:T(8,128)(2,1)S(1)}, bf16[1,8,1,10,256]{4,1,3,2,0:T(8,128)(2,1)S(1)}, u32[]{:S(2)}, u32[]{:S(2)}) collective-permute-start(bf16[1,8,1,10,256]{4,1,3,2,0:T(8,128)(2,1)S(1)} %get-tuple-element.38), channel_id=1, source_target_pairs={{0,8},{8,16},{16,24},{24,32},{32,40},{40,48},{48,56},{1,9},{9,17},... | collective-permute-start | bytes 122888 | tf_op jit(solution)/shard_map/ppermute | solution.py:17
  43.9 6.9 %collective-permute-start.5 = (bf16[1,8,1,10,256]{4,1,3,2,0:T(8,128)(2,1)S(1)}, bf16[1,8,1,10,256]{4,1,3,2,0:T(8,128)(2,1)S(1)}, u32[]{:S(2)}, u32[]{:S(2)}) collective-permute-start(bf16[1,8,1,10,256]{4,1,3,2,0:T(8,128)(2,1)S(1)} %get-tuple-element.39), channel_id=1, source_target_pairs={{8,0},{16,8},{24,16},{32,24},{40,32},{48,40},{56,48},{9,1},{17,9},... | collective-permute-start | bytes 122888 | tf_op jit(solution)/shard_map/ppermute | solution.py:20
  51.4 7.0 %collective-permute-start.6 = (bf16[1,8,12,1,256]{4,1,3,2,0:T(8,128)(2,1)}, bf16[1,8,12,1,256]{4,1,3,2,0:T(8,128)(2,1)S(1)}, u32[]{:S(2)}, u32[]{:S(2)}) collective-permute-start(bf16[1,8,12,1,256]{4,1,3,2,0:T(8,128)(2,1)} %get-tuple-element.34), channel_id=1, source_target_pairs={{0,1},{1,2},{2,3},{3,4},{4,5},{5,6},{6,7},{8,9},{9,10},{10,11},{11... | collective-permute-start | bytes 147464 | tf_op jit(solution)/shard_map/ppermute | solution.py:17
  53.4 9.8 %collective-permute-start.7 = (bf16[1,8,12,1,256]{4,1,3,2,0:T(8,128)(2,1)}, bf16[1,8,12,1,256]{4,1,3,2,0:T(8,128)(2,1)S(1)}, u32[]{:S(2)}, u32[]{:S(2)}) collective-permute-start(bf16[1,8,12,1,256]{4,1,3,2,0:T(8,128)(2,1)} %get-tuple-element.35), channel_id=1, source_target_pairs={{1,0},{2,1},{3,2},{4,3},{5,4},{6,5},{7,6},{9,8},{10,9},{11,10},{12... | collective-permute-start | bytes 147464 | tf_op jit(solution)/shard_map/ppermute | solution.py:20
  64.6 1.1 copy-start.14
  65.6 1.7 copy-start.10
  65.6 1.7 copy-start.17
  109.5 16.4 %all-to-all-start.1 = ((bf16[8,1,1,10,10,512]{5,4,3,2,1,0:T(8,128)(2,1)}), bf16[8,1,1,10,10,512]{5,4,3,2,1,0:T(8,128)(2,1)}, u32[]{:S(2)}, u32[]{:S(2)}) async-start(bf16[8,1,1,10,10,512]{5,4,3,2,1,0:T(8,128)(2,1)} %fusion.139), calls=%async_computation.1 | async-start | bytes 2621440 | tf_op jit(solution)/shard_map/all_to_all | solution.py:80
  132.4 2.8 %copy-start.16 = (bf16[512,768]{1,0:T(8,128)(2,1)S(1)}, bf16[512,768]{1,0:T(8,128)(2,1)}, u32[]{:S(2)}) copy-start(bf16[512,768]{1,0:T(8,128)(2,1)} %param.15) | copy-start | bytes 2359300
  137.8 7.6 %copy-start.3 = (f32[1,1,10,8,10,512]{5,1,4,3,2,0:T(1,128)S(1)}, f32[1,1,10,8,10,512]{5,1,4,3,2,0:T(1,128)}, u32[]{:S(2)}) copy-start(f32[1,1,10,8,10,512]{5,1,4,3,2,0:T(1,128)} %copy.195) | copy-start | bytes 4915204
  138.6 8.2 %collective-permute-start.8 = (bf16[1,1,1,80,768]{4,3,2,1,0:T(8,128)(2,1)S(1)}, bf16[1,1,1,80,768]{4,3,2,1,0:T(8,128)(2,1)S(1)}, u32[]{:S(2)}, u32[]{:S(2)}) collective-permute-start(bf16[1,1,1,80,768]{4,3,2,1,0:T(8,128)(2,1)S(1)} %get-tuple-element.5), channel_id=1, source_target_pairs={{0,1},{1,2},{2,3},{3,4},{4,5},{5,6},{6,7},{8,9},{9,10},{10,11},{11... | collective-permute-start | bytes 368648 | tf_op jit(solution)/shard_map/ppermute | solution.py:17
  143.2 10.4 %collective-permute-start.9 = (bf16[1,1,1,80,768]{4,3,2,1,0:T(8,128)(2,1)S(1)}, bf16[1,1,1,80,768]{4,3,2,1,0:T(8,128)(2,1)S(1)}, u32[]{:S(2)}, u32[]{:S(2)}) collective-permute-start(bf16[1,1,1,80,768]{4,3,2,1,0:T(8,128)(2,1)S(1)} %get-tuple-element.6), channel_id=1, source_target_pairs={{1,0},{2,1},{3,2},{4,3},{5,4},{6,5},{7,6},{9,8},{10,9},{11,10},{12... | collective-permute-start | bytes 368648 | tf_op jit(solution)/shard_map/ppermute | solution.py:20
  189.8 11.7 %copy-start.8 = (bf16[1,5,40,768]{3,2,1,0:T(8,128)(2,1)S(1)}, bf16[1,5,40,768]{3,2,1,0:T(8,128)(2,1)}, u32[]{:S(2)}) copy-start(bf16[1,5,40,768]{3,2,1,0:T(8,128)(2,1)} %slice.179) | copy-start | bytes 921604
  202.2 7.5 %copy-start.7 = (bf16[1,5,40,1,6,128]{5,4,2,1,3,0:T(8,128)(2,1)S(1)}, bf16[1,5,40,1,6,128]{5,4,2,1,3,0:T(8,128)(2,1)}, u32[]{:S(2)}) copy-start(bf16[1,5,40,1,6,128]{5,4,2,1,3,0:T(8,128)(2,1)} %stack.181) | copy-start | bytes 921604
  202.2 8.3 %copy-start.5 = (bf16[1,5,40,1,6,128]{5,4,2,1,3,0:T(8,128)(2,1)S(1)}, bf16[1,5,40,1,6,128]{5,4,2,1,3,0:T(8,128)(2,1)}, u32[]{:S(2)}) copy-start(bf16[1,5,40,1,6,128]{5,4,2,1,3,0:T(8,128)(2,1)} %stack.182) | copy-start | bytes 921604
  204.1 8.7 %copy-start.2 = (bf16[9,128,6,128]{3,2,1,0:T(8,128)(2,1)S(1)}, bf16[9,128,6,128]{3,2,1,0:T(8,128)(2,1)}, u32[]{:S(2)}) copy-start(bf16[9,128,6,128]{3,2,1,0:T(8,128)(2,1)} %reshape.595) | copy-start | bytes 5308420
  218.1 9.2 %collective-permute-start.10 = (bf16[1,1,1,40,768]{4,3,2,1,0:T(8,128)(2,1)S(1)}, bf16[1,1,1,40,768]{4,3,2,1,0:T(8,128)(2,1)S(1)}, u32[]{:S(2)}, u32[]{:S(2)}) collective-permute-start(bf16[1,1,1,40,768]{4,3,2,1,0:T(8,128)(2,1)S(1)} %get-tuple-element.42), channel_id=1, source_target_pairs={{0,1},{1,2},{2,3},{3,4},{4,5},{5,6},{6,7},{8,9},{9,10},{10,11},{11... | collective-permute-start | bytes 184328 | tf_op jit(solution)/shard_map/ppermute | solution.py:17
  220.0 9.7 %collective-permute-start.11 = (bf16[1,1,1,40,768]{4,3,2,1,0:T(8,128)(2,1)S(1)}, bf16[1,1,1,40,768]{4,3,2,1,0:T(8,128)(2,1)S(1)}, u32[]{:S(2)}, u32[]{:S(2)}) collective-permute-start(bf16[1,1,1,40,768]{4,3,2,1,0:T(8,128)(2,1)S(1)} %get-tuple-element.43), channel_id=1, source_target_pairs={{1,0},{2,1},{3,2},{4,3},{5,4},{6,5},{7,6},{9,8},{10,9},{11,10},{12... | collective-permute-start | bytes 184328 | tf_op jit(solution)/shard_map/ppermute | solution.py:20
  233.5 10.5 %copy-start.9 = (bf16[1,5,40,768]{3,2,1,0:T(8,128)(2,1)S(1)}, bf16[1,5,40,768]{3,2,1,0:T(8,128)(2,1)}, u32[]{:S(2)}) copy-start(bf16[1,5,40,768]{3,2,1,0:T(8,128)(2,1)} %get-tuple-element.27) | copy-start | bytes 921604
  245.8 7.5 %copy-start.6 = (bf16[1,5,40,1,6,128]{5,4,2,1,3,0:T(8,128)(2,1)S(1)}, bf16[1,5,40,1,6,128]{5,4,2,1,3,0:T(8,128)(2,1)}, u32[]{:S(2)}) copy-start(bf16[1,5,40,1,6,128]{5,4,2,1,3,0:T(8,128)(2,1)} %stack.191) | copy-start | bytes 921604
  245.8 8.3 %copy-start.4 = (bf16[1,5,40,1,6,128]{5,4,2,1,3,0:T(8,128)(2,1)S(1)}, bf16[1,5,40,1,6,128]{5,4,2,1,3,0:T(8,128)(2,1)}, u32[]{:S(2)}) copy-start(bf16[1,5,40,1,6,128]{5,4,2,1,3,0:T(8,128)(2,1)} %stack.192) | copy-start | bytes 921604
  247.7 8.8 %copy-start.1 = (bf16[9,128,6,128]{3,2,1,0:T(8,128)(2,1)S(1)}, bf16[9,128,6,128]{3,2,1,0:T(8,128)(2,1)}, u32[]{:S(2)}) copy-start(bf16[9,128,6,128]{3,2,1,0:T(8,128)(2,1)} %reshape.599) | copy-start | bytes 5308420
